TPU v7x, 512 devices: a whole 4x8x8 slice. The times are simulated.
512 devices in a mesh: rows: 64 (over y, x, core), dates: 8 (over z).
Axes of the slice: x: 4, y: 8, z: 8, core: 2. Of those that a mesh axis runs over, the one named last changes fastest.
Arguments:
- obs_mask: int32 [16, 512, 4096], P('dates', 'rows'), may hold values 0 or 1
- precision: float32 [16, 512, 4096], P('dates', 'rows'), may hold values from 0.5 to 4
- observed: float32 [16, 512, 4096], P('dates', 'rows')
- edge_class: int32 [2, 512, 4096], P(None, 'rows'), may hold values from 0 to 7
- temporal_weight: float32 [15], replicated, may hold values from 0.5 to 4
- inverse: bfloat16 [16, 16, 512, 4096], P(None, None, 'rows', 'dates'), as said below
Outputs:
- solution: float32 [16, 512, 4096], P('dates', 'rows')
- residual: float32 [16, 512, 4096], P('dates', 'rows')
Inputs may be any that keep to these rules, and one draw needn't show every extreme that they name: `inverse`: each pixel's matrix is symmetric with a diagonal larger than the sum of magnitudes of its row's other entries.
All inputs are finite; a program needn't handle non-finite values. No bound on the sum of `obs_mask` on one device may be relied on, other than what follows from the above.
Results may differ from a plain program's by a relative error of at most 0.0065.
Values sent between devices are 32-bit elements; how exact they have to be, the bound alone decides.
A program may use at most 64 MiB of HBM per device.

v0:
```python
import jax
import jax.numpy as jnp
from jax import lax
from jax.sharding import PartitionSpec as P

mass_term = 0.1


def shifted(value, axis, steps):
    count = lax.axis_size(axis)
    first, last = (max(0, -steps), min(count, count - steps))
    return lax.ppermute(value, axis, [(i, i + steps) for i in range(first, last)])


def apply_inverse(inverse, values):
    total = inverse[:, 0].astype(jnp.float32) * values[0][None]
    for source in range(1, values.shape[0]):
        total = total + inverse[:, source].astype(jnp.float32) * values[source][None]
    return total


def body(obs_mask, precision, observed, edge_class, temporal_weight, inverse):
    dates_here, rows_here, columns = observed.shape
    cols_here = inverse.shape[3]
    line_start = lax.axis_index("rows") * rows_here
    lines_total = rows_here * lax.axis_size("rows")
    col_start = lax.axis_index("dates") * cols_here

    weight = obs_mask.astype(jnp.float32) * precision
    both = jnp.stack([weight, weight * observed])
    both = lax.all_to_all(both, "dates", split_axis=3, concat_axis=1, tiled=True)
    weight, rhs = both[0], both[1]

    classes = 0.25 * (edge_class.astype(jnp.float32) + 1.0)
    col_ids = lax.broadcasted_iota(jnp.int32, (rows_here, columns), 1)
    row_ids = lax.broadcasted_iota(jnp.int32, (rows_here, cols_here), 0) + line_start
    across_all = jnp.where(col_ids == columns - 1, 0.0, classes[0])
    across_ext = jnp.pad(across_all, ((0, 0), (1, 0)))
    across_prev = lax.dynamic_slice_in_dim(across_ext, col_start, cols_here, 1)
    across = lax.dynamic_slice_in_dim(across_all, col_start, cols_here, 1)
    downward = lax.dynamic_slice_in_dim(classes[1], col_start, cols_here, 1)
    downward = jnp.where(row_ids == lines_total - 1, 0.0, downward)
    downward_prev = jnp.concatenate([shifted(downward[-1:], "rows", 1), downward[:-1]], axis=0)
    zero_one = jnp.zeros((1,), jnp.float32)
    tau_up = jnp.concatenate([temporal_weight, zero_one])[:, None, None]
    tau_down = jnp.concatenate([zero_one, temporal_weight])[:, None, None]
    centre = (
        mass_term + weight + (across + across_prev + downward + downward_prev)[None]
        + (tau_up + tau_down)
    )

    def operator(field):
        above = jnp.concatenate([shifted(field[:, -1:], "rows", 1), field[:, :-1]], axis=1)
        below = jnp.concatenate([field[:, 1:], shifted(field[:, :1], "rows", -1)], axis=1)
        left = jnp.concatenate([shifted(field[:, :, -1:], "dates", 1), field[:, :, :-1]], axis=2)
        right = jnp.concatenate([field[:, :, 1:], shifted(field[:, :, :1], "dates", -1)], axis=2)
        before = jnp.pad(field, ((1, 0), (0, 0), (0, 0)))[:-1]
        after = jnp.pad(field, ((0, 1), (0, 0), (0, 0)))[1:]
        return (
            centre * field
            - (across * right + across_prev * left)
            - (downward * below + downward_prev * above)
            - (tau_up * after + tau_down * before)
        )

    precond = apply_inverse(inverse, rhs)
    image = operator(precond)
    mapped = apply_inverse(inverse, image)
    mapped_image = operator(mapped)
    sums = jnp.stack(
        [
            jnp.sum(rhs * precond),
            jnp.sum(precond * image),
            jnp.sum(image * mapped),
            jnp.sum(mapped * mapped_image),
        ]
    )
    sums = lax.psum(sums, ("rows", "dates"))
    rz, dd, ee, ff = sums[0], sums[1], sums[2], sums[3]
    alpha = rz / dd
    grown = alpha * ee / dd
    alpha_next = (alpha * alpha * ee - rz) / (alpha * alpha * (ff - ee * ee / dd))
    first = alpha + alpha_next * grown
    second = alpha_next * alpha
    out = jnp.stack([first * precond - second * mapped, rhs - first * image + second * mapped_image])
    out = lax.all_to_all(out, "dates", split_axis=1, concat_axis=3, tiled=True)
    return out[0], out[1]


def solution(mesh):
    return jax.shard_map(
        body,
        mesh=mesh,
        in_specs=(
            P("dates", "rows", None),
            P("dates", "rows", None),
            P("dates", "rows", None),
            P(None, "rows", None),
            P(),
            P(None, None, "rows", "dates"),
        ),
        out_specs=(P("dates", "rows", None), P("dates", "rows", None)),
        check_vma=False,
    )
```

profile of v0, /device:TPU:1, one launch (start us, length us, event | category | flops | bytes accessed | tf_op | source)
XLA Modules:
  0.0 246.7 jit_solution(16082085440796772396)
XLA Ops:
  0.6 1.2 fusion.82
  1.8 8.2 %copy.156 = f32[2,2,8,4096]{2,1,0,3:T(2,128)} copy(f32[2,2,8,4096]{3,2,1,0:T(8,128)S(1)} %pad_maximum_fusion) | data formatting | bytes 1048576 | tf_op jit(solution)/shard_map/stack | solution.py:30
  10.0 15.6 %reshape.805 = f32[8,1,16384]{2,1,0:T(1,128)} reshape(f32[4096,2,2,8]{3,2,1,0:T(2,128)} %bitcast.617) | data formatting | bytes 1048576
  25.7 11.0 %all-to-all-start = ((f32[8,1,16384]{2,1,0:T(1,128)}), f32[8,1,16384]{2,1,0:T(1,128)S(1)}, u32[]{:S(2)}, u32[]{:S(2)}) async-start(f32[8,1,16384]{2,1,0:T(1,128)} %reshape.805), calls=%async_computation | async-start | bytes 1048576 | tf_op jit(solution)/shard_map/all_to_all | solution.py:31
  36.8 0.1 bitcast_select_fusion
  36.8 4.1 %collective-permute-start = (f32[1,512]{1,0:T(1,128)S(1)}, f32[1,512]{1,0:T(1,128)S(1)}, u32[]{:S(2)}, u32[]{:S(2)}) collective-permute-start(f32[1,512]{1,0:T(1,128)S(1)} %slice.360), channel_id=1, source_target_pairs={{0,8},{8,16},{16,24},{24,32},{32,40},{40,48},{48,56},{56,64},{64,7... | collective-permute-start | bytes 6152 | tf_op jit(solution)/shard_map/ppermute | solution.py:12
  41.0 0.7 select_bitcast_fusion
  41.7 1.9 bitcast_convert_fusion.15
  43.6 0.7 fusion.83
  44.3 0.7 add_add_fusion
  45.0 9.6 %all-to-all-done = f32[8,1,16384]{2,1,0:T(1,128)S(1)} async-done(((f32[8,1,16384]{2,1,0:T(1,128)}), f32[8,1,16384]{2,1,0:T(1,128)S(1)}, u32[]{:S(2)}, u32[]{:S(2)}) %all-to-all-start) | async-done | bytes 524320 | tf_op jit(solution)/shard_map/all_to_all | solution.py:31
  54.6 0.5 broadcast.381
  55.1 1.9 reduce.1
  57.0 16.0 %reshape.806 = f32[4096,2,2,8]{3,2,1,0:T(2,128)} reshape(f32[8,16384]{1,0:T(8,128)S(1)} %reduce.1) | data formatting | bytes 1048576
  73.0 10.1 %copy.158 = f32[2,2,8,8,512]{4,2,1,3,0:T(8,128)S(1)} copy(f32[2,2,8,8,512]{2,1,0,4,3:T(2,128)} %bitcast.618) | data formatting | bytes 1048576 | tf_op jit(solution)/shard_map/all_to_all | solution.py:31
  83.3 0.0 copy-start.1
  83.3 0.0 copy-start.2
  83.5 0.4 fusion.51
  83.9 0.1 fusion.91
  83.9 0.1 fusion.92
  84.1 1.4 collective-permute-start.1
  85.5 4.0 %collective-permute-start.2 = (f32[16,8,1]{2,1,0:T(8,128)S(1)}, f32[16,8,1]{2,1,0:T(8,128)S(1)}, u32[]{:S(2)}, u32[]{:S(2)}) collective-permute-start(f32[16,8,1]{2,1,0:T(8,128)S(1)} %get-tuple-element.60), channel_id=1, source_target_pairs={{0,1},{1,2},{2,3},{3,4},{4,5},{5,6},{6,7},{8,9},{9,10},{10,11},{11... | collective-permute-start | bytes 1544 | tf_op jit(solution)/shard_map/ppermute | solution.py:12
  89.5 3.0 %collective-permute-start.3 = (f32[16,1,512]{2,1,0:T(1,128)S(1)}, f32[16,1,512]{2,1,0:T(1,128)S(1)}, u32[]{:S(2)}, u32[]{:S(2)}) collective-permute-start(f32[16,1,512]{2,1,0:T(1,128)S(1)} %get-tuple-element.57), channel_id=1, source_target_pairs={{8,0},{16,8},{24,16},{32,24},{40,32},{48,40},{56,48},{64,56},{72,6... | collective-permute-start | bytes 98312 | tf_op jit(solution)/shard_map/ppermute | solution.py:12
  92.5 3.0 %collective-permute-start.4 = (f32[16,1,512]{2,1,0:T(1,128)S(1)}, f32[16,1,512]{2,1,0:T(1,128)S(1)}, u32[]{:S(2)}, u32[]{:S(2)}) collective-permute-start(f32[16,1,512]{2,1,0:T(1,128)S(1)} %get-tuple-element.56), channel_id=1, source_target_pairs={{0,8},{8,16},{16,24},{24,32},{32,40},{40,48},{48,56},{56,64},{64,7... | collective-permute-start | bytes 98312 | tf_op jit(solution)/shard_map/ppermute | solution.py:12
  95.7 1.2 multiply_reduce_fusion.3
  97.0 0.1 fusion.93
  97.1 0.0 collective-permute-done.2
  97.1 0.0 collective-permute-done.3
  97.2 0.3 fusion.2
  97.6 0.4 fusion.52
  98.0 0.1 fusion.86
  98.1 0.1 fusion.87
  98.3 1.3 collective-permute-start.5
  99.6 4.0 %collective-permute-start.6 = (f32[16,8,1]{2,1,0:T(8,128)S(1)}, f32[16,8,1]{2,1,0:T(8,128)S(1)}, u32[]{:S(2)}, u32[]{:S(2)}) collective-permute-start(f32[16,8,1]{2,1,0:T(8,128)S(1)} %get-tuple-element.35), channel_id=1, source_target_pairs={{0,1},{1,2},{2,3},{3,4},{4,5},{5,6},{6,7},{8,9},{9,10},{10,11},{11... | collective-permute-start | bytes 1544 | tf_op jit(solution)/shard_map/ppermute | solution.py:12
  103.6 1.9 collective-permute-start.7
  105.5 4.4 %collective-permute-start.8 = (f32[16,1,512]{2,1,0:T(1,128)S(1)}, f32[16,1,512]{2,1,0:T(1,128)S(1)}, u32[]{:S(2)}, u32[]{:S(2)}) collective-permute-start(f32[16,1,512]{2,1,0:T(1,128)S(1)} %get-tuple-element.39), channel_id=1, source_target_pairs={{0,8},{8,16},{16,24},{24,32},{32,40},{40,48},{48,56},{56,64},{64,7... | collective-permute-start | bytes 98312 | tf_op jit(solution)/shard_map/ppermute | solution.py:12
  109.9 0.1 fusion.88
  109.9 0.0 collective-permute-done.5
  109.9 0.7 collective-permute-done.8
  110.7 1.5 multiply_reduce_fusion.2
  112.2 2.6 %pad_maximum_fusion.5 = f32[4]{0:T(128)S(1)} fusion(f32[1]{0:T(128)} %bitcast.76, f32[1]{0:T(128)} %bitcast.75, f32[1]{0:T(128)} %bitcast.58, f32[1]{0:T(128)} %bitcast.37), kind=kLoop, calls=%fused_computation.229 | loop fusion | flops 12 | bytes 32 | tf_op jit(solution)/shard_map/stack | solution.py:70
  114.8 103.1 %psum.7 = f32[4]{0:T(128)S(1)} all-reduce(f32[4]{0:T(128)S(1)} %pad_maximum_fusion.5), channel_id=1, replica_groups=mesh['rows'=64,'dates'=8] {'rows','dates'}, use_global_device_ids=true, to_apply=%region_4.5 | all-reduce | flops 4 | bytes 32 | tf_op jit(solution)/shard_map/psum | solution.py:78
  217.9 0.6 fusion.94
  225.0 1.6 fusion.19
  226.6 0.1 add_bitcast_fusion
  226.7 18.4 %all_to_all.30 = f32[2,16,8,512]{3,2,0,1:T(8,128)S(1)} all-to-all(f32[2,16,8,512]{3,2,0,1:T(8,128)S(1)} %pad_maximum_fusion.1), channel_id=1, replica_groups=mesh['rows'=64,'dates'=8] {'dates'}, dimensions={1} | all-to-all | bytes 1048576 | tf_op jit(solution)/shard_map/all_to_all | solution.py:86
  245.2 0.7 copy.176
  245.9 0.7 copy.177
  (83 shorter events, 0.5 us)
Async XLA Ops:
  10.0 26.6 %copy-start.23 = (s32[2,8,4096]{2,1,0:T(8,128)S(1)}, s32[2,8,4096]{2,1,0:T(8,128)}, u32[]{:S(2)}) copy-start(s32[2,8,4096]{2,1,0:T(8,128)} %param.9) | copy-start | bytes 786436
  25.7 16.0 %copy-start = (bf16[16,16,8,512]{3,2,1,0:T(8,128)(2,1)S(1)}, bf16[16,16,8,512]{3,2,1,0:T(8,128)(2,1)}, u32[]{:S(2)}) copy-start(bf16[16,16,8,512]{3,2,1,0:T(8,128)(2,1)} %param.11) | copy-start | bytes 6291460
  25.7 29.0 %all-to-all-start = ((f32[8,1,16384]{2,1,0:T(1,128)}), f32[8,1,16384]{2,1,0:T(1,128)S(1)}, u32[]{:S(2)}, u32[]{:S(2)}) async-start(f32[8,1,16384]{2,1,0:T(1,128)} %reshape.805), calls=%async_computation | async-start | bytes 1048576 | tf_op jit(solution)/shard_map/all_to_all | solution.py:31
  36.8 7.5 %collective-permute-start = (f32[1,512]{1,0:T(1,128)S(1)}, f32[1,512]{1,0:T(1,128)S(1)}, u32[]{:S(2)}, u32[]{:S(2)}) collective-permute-start(f32[1,512]{1,0:T(1,128)S(1)} %slice.360), channel_id=1, source_target_pairs={{0,8},{8,16},{16,24},{24,32},{32,40},{40,48},{48,56},{56,64},{64,7... | collective-permute-start | bytes 6152 | tf_op jit(solution)/shard_map/ppermute | solution.py:12
  41.7 1.9 copy-start.32
  83.2 27.4 %copy-start.16 = (f32[8,512]{1,0:T(8,128)}, f32[8,512]{1,0:T(8,128)S(1)}, u32[]{:S(2)}) copy-start(f32[8,512]{1,0:T(8,128)S(1)} %get-tuple-element.73) | copy-start | bytes 49156
  83.2 27.4 %copy-start.17 = (f32[8,512]{1,0:T(8,128)}, f32[8,512]{1,0:T(8,128)S(1)}, u32[]{:S(2)}) copy-start(f32[8,512]{1,0:T(8,128)S(1)} %get-tuple-element.74) | copy-start | bytes 49156
  83.3 27.4 %copy-start.18 = (f32[8,512]{1,0:T(8,128)}, f32[8,512]{1,0:T(8,128)S(1)}, u32[]{:S(2)}) copy-start(f32[8,512]{1,0:T(8,128)S(1)} %get-tuple-element.75) | copy-start | bytes 49156
  83.3 27.4 %copy-start.19 = (f32[8,512]{1,0:T(8,128)}, f32[8,512]{1,0:T(8,128)S(1)}, u32[]{:S(2)}) copy-start(f32[8,512]{1,0:T(8,128)S(1)} %get-tuple-element.76) | copy-start | bytes 49156
  83.3 27.4 %copy-start.20 = (f32[8,512]{1,0:T(8,128)}, f32[8,512]{1,0:T(8,128)S(1)}, u32[]{:S(2)}) copy-start(f32[8,512]{1,0:T(8,128)S(1)} %get-tuple-element.77) | copy-start | bytes 49156
  83.3 27.4 %copy-start.21 = (f32[8,512]{1,0:T(8,128)}, f32[8,512]{1,0:T(8,128)S(1)}, u32[]{:S(2)}) copy-start(f32[8,512]{1,0:T(8,128)S(1)} %get-tuple-element.78) | copy-start | bytes 49156
  83.3 27.4 %copy-start.22 = (f32[8,512]{1,0:T(8,128)}, f32[8,512]{1,0:T(8,128)S(1)}, u32[]{:S(2)}) copy-start(f32[8,512]{1,0:T(8,128)S(1)} %get-tuple-element.79) | copy-start | bytes 49156
  83.3 12.2 %copy-start.1 = (f32[16,1,8,512]{3,2,0,1:T(8,128)S(1)}, f32[16,1,8,512]{3,2,0,1:T(8,128)}, u32[]{:S(2)}) copy-start(f32[16,1,8,512]{3,2,0,1:T(8,128)} %get-tuple-element.11) | copy-start | bytes 786436
  83.3 12.2 %copy-start.2 = (f32[16,1,8,512]{3,2,0,1:T(8,128)S(1)}, f32[16,1,8,512]{3,2,0,1:T(8,128)}, u32[]{:S(2)}) copy-start(f32[16,1,8,512]{3,2,0,1:T(8,128)} %get-tuple-element.12) | copy-start | bytes 786436
  83.3 12.2 %copy-start.3 = (f32[16,1,8,512]{3,2,0,1:T(8,128)S(1)}, f32[16,1,8,512]{3,2,0,1:T(8,128)}, u32[]{:S(2)}) copy-start(f32[16,1,8,512]{3,2,0,1:T(8,128)} %get-tuple-element.13) | copy-start | bytes 786436
  83.3 12.2 %copy-start.4 = (f32[16,1,8,512]{3,2,0,1:T(8,128)S(1)}, f32[16,1,8,512]{3,2,0,1:T(8,128)}, u32[]{:S(2)}) copy-start(f32[16,1,8,512]{3,2,0,1:T(8,128)} %get-tuple-element.14) | copy-start | bytes 786436
  83.4 12.2 %copy-start.5 = (f32[16,1,8,512]{3,2,0,1:T(8,128)S(1)}, f32[16,1,8,512]{3,2,0,1:T(8,128)}, u32[]{:S(2)}) copy-start(f32[16,1,8,512]{3,2,0,1:T(8,128)} %get-tuple-element.15) | copy-start | bytes 786436
  83.4 12.2 %copy-start.6 = (f32[16,1,8,512]{3,2,0,1:T(8,128)S(1)}, f32[16,1,8,512]{3,2,0,1:T(8,128)}, u32[]{:S(2)}) copy-start(f32[16,1,8,512]{3,2,0,1:T(8,128)} %get-tuple-element.16) | copy-start | bytes 786436
  83.4 12.2 %copy-start.7 = (f32[16,1,8,512]{3,2,0,1:T(8,128)S(1)}, f32[16,1,8,512]{3,2,0,1:T(8,128)}, u32[]{:S(2)}) copy-start(f32[16,1,8,512]{3,2,0,1:T(8,128)} %get-tuple-element.17) | copy-start | bytes 786436
  83.4 12.2 %copy-start.8 = (f32[16,1,8,512]{3,2,0,1:T(8,128)S(1)}, f32[16,1,8,512]{3,2,0,1:T(8,128)}, u32[]{:S(2)}) copy-start(f32[16,1,8,512]{3,2,0,1:T(8,128)} %get-tuple-element.18) | copy-start | bytes 786436
  83.4 12.2 %copy-start.9 = (f32[16,1,8,512]{3,2,0,1:T(8,128)S(1)}, f32[16,1,8,512]{3,2,0,1:T(8,128)}, u32[]{:S(2)}) copy-start(f32[16,1,8,512]{3,2,0,1:T(8,128)} %get-tuple-element.19) | copy-start | bytes 786436
  83.4 12.2 %copy-start.10 = (f32[16,1,8,512]{3,2,0,1:T(8,128)S(1)}, f32[16,1,8,512]{3,2,0,1:T(8,128)}, u32[]{:S(2)}) copy-start(f32[16,1,8,512]{3,2,0,1:T(8,128)} %get-tuple-element.20) | copy-start | bytes 786436
  83.4 12.2 %copy-start.11 = (f32[16,1,8,512]{3,2,0,1:T(8,128)S(1)}, f32[16,1,8,512]{3,2,0,1:T(8,128)}, u32[]{:S(2)}) copy-start(f32[16,1,8,512]{3,2,0,1:T(8,128)} %get-tuple-element.21) | copy-start | bytes 786436
  83.4 12.2 %copy-start.12 = (f32[16,1,8,512]{3,2,0,1:T(8,128)S(1)}, f32[16,1,8,512]{3,2,0,1:T(8,128)}, u32[]{:S(2)}) copy-start(f32[16,1,8,512]{3,2,0,1:T(8,128)} %get-tuple-element.22) | copy-start | bytes 786436
  83.4 12.2 %copy-start.13 = (f32[16,1,8,512]{3,2,0,1:T(8,128)S(1)}, f32[16,1,8,512]{3,2,0,1:T(8,128)}, u32[]{:S(2)}) copy-start(f32[16,1,8,512]{3,2,0,1:T(8,128)} %get-tuple-element.23) | copy-start | bytes 786436
  83.4 12.2 %copy-start.14 = (f32[16,1,8,512]{3,2,0,1:T(8,128)S(1)}, f32[16,1,8,512]{3,2,0,1:T(8,128)}, u32[]{:S(2)}) copy-start(f32[16,1,8,512]{3,2,0,1:T(8,128)} %get-tuple-element.24) | copy-start | bytes 786436
  83.5 12.2 %copy-start.15 = (f32[16,1,8,512]{3,2,0,1:T(8,128)S(1)}, f32[16,1,8,512]{3,2,0,1:T(8,128)}, u32[]{:S(2)}) copy-start(f32[16,1,8,512]{3,2,0,1:T(8,128)} %get-tuple-element.25) | copy-start | bytes 786436
  84.1 13.0 %collective-permute-start.1 = (f32[16,8,1]{2,1,0:T(8,128)S(1)}, f32[16,8,1]{2,1,0:T(8,128)S(1)}, u32[]{:S(2)}, u32[]{:S(2)}) collective-permute-start(f32[16,8,1]{2,1,0:T(8,128)S(1)} %get-tuple-element.61), channel_id=1, source_target_pairs={{1,0},{2,1},{3,2},{4,3},{5,4},{6,5},{7,6},{9,8},{10,9},{11,10},{12... | collective-permute-start | bytes 1544 | tf_op jit(solution)/shard_map/ppermute | solution.py:12
  85.5 11.6 %collective-permute-start.2 = (f32[16,8,1]{2,1,0:T(8,128)S(1)}, f32[16,8,1]{2,1,0:T(8,128)S(1)}, u32[]{:S(2)}, u32[]{:S(2)}) collective-permute-start(f32[16,8,1]{2,1,0:T(8,128)S(1)} %get-tuple-element.60), channel_id=1, source_target_pairs={{0,1},{1,2},{2,3},{3,4},{4,5},{5,6},{6,7},{8,9},{9,10},{10,11},{11... | collective-permute-start | bytes 1544 | tf_op jit(solution)/shard_map/ppermute | solution.py:12
  89.5 7.6 %collective-permute-start.3 = (f32[16,1,512]{2,1,0:T(1,128)S(1)}, f32[16,1,512]{2,1,0:T(1,128)S(1)}, u32[]{:S(2)}, u32[]{:S(2)}) collective-permute-start(f32[16,1,512]{2,1,0:T(1,128)S(1)} %get-tuple-element.57), channel_id=1, source_target_pairs={{8,0},{16,8},{24,16},{32,24},{40,32},{48,40},{56,48},{64,56},{72,6... | collective-permute-start | bytes 98312 | tf_op jit(solution)/shard_map/ppermute | solution.py:12
  92.5 4.6 %collective-permute-start.4 = (f32[16,1,512]{2,1,0:T(1,128)S(1)}, f32[16,1,512]{2,1,0:T(1,128)S(1)}, u32[]{:S(2)}, u32[]{:S(2)}) collective-permute-start(f32[16,1,512]{2,1,0:T(1,128)S(1)} %get-tuple-element.56), channel_id=1, source_target_pairs={{0,8},{8,16},{16,24},{24,32},{32,40},{40,48},{48,56},{56,64},{64,7... | collective-permute-start | bytes 98312 | tf_op jit(solution)/shard_map/ppermute | solution.py:12
  95.7 1.5 copy-start.24
  95.7 1.5 copy-start.25
  95.7 1.5 copy-start.26
  95.7 1.5 copy-start.27
  95.7 1.5 copy-start.28
  95.7 1.5 copy-start.29
  95.7 1.5 copy-start.30
  95.7 1.5 copy-start.31
  98.3 11.7 %collective-permute-start.5 = (f32[16,8,1]{2,1,0:T(8,128)S(1)}, f32[16,8,1]{2,1,0:T(8,128)S(1)}, u32[]{:S(2)}, u32[]{:S(2)}) collective-permute-start(f32[16,8,1]{2,1,0:T(8,128)S(1)} %get-tuple-element.34), channel_id=1, source_target_pairs={{1,0},{2,1},{3,2},{4,3},{5,4},{6,5},{7,6},{9,8},{10,9},{11,10},{12... | collective-permute-start | bytes 1544 | tf_op jit(solution)/shard_map/ppermute | solution.py:12
  99.6 10.4 %collective-permute-start.6 = (f32[16,8,1]{2,1,0:T(8,128)S(1)}, f32[16,8,1]{2,1,0:T(8,128)S(1)}, u32[]{:S(2)}, u32[]{:S(2)}) collective-permute-start(f32[16,8,1]{2,1,0:T(8,128)S(1)} %get-tuple-element.35), channel_id=1, source_target_pairs={{0,1},{1,2},{2,3},{3,4},{4,5},{5,6},{6,7},{8,9},{9,10},{10,11},{11... | collective-permute-start | bytes 1544 | tf_op jit(solution)/shard_map/ppermute | solution.py:12
  103.6 6.4 %collective-permute-start.7 = (f32[16,1,512]{2,1,0:T(1,128)S(1)}, f32[16,1,512]{2,1,0:T(1,128)S(1)}, u32[]{:S(2)}, u32[]{:S(2)}) collective-permute-start(f32[16,1,512]{2,1,0:T(1,128)S(1)} %get-tuple-element.38), channel_id=1, source_target_pairs={{8,0},{16,8},{24,16},{32,24},{40,32},{48,40},{56,48},{64,56},{72,6... | collective-permute-start | bytes 98312 | tf_op jit(solution)/shard_map/ppermute | solution.py:12
  105.5 5.1 %collective-permute-start.8 = (f32[16,1,512]{2,1,0:T(1,128)S(1)}, f32[16,1,512]{2,1,0:T(1,128)S(1)}, u32[]{:S(2)}, u32[]{:S(2)}) collective-permute-start(f32[16,1,512]{2,1,0:T(1,128)S(1)} %get-tuple-element.39), channel_id=1, source_target_pairs={{0,8},{8,16},{16,24},{24,32},{32,40},{40,48},{48,56},{56,64},{64,7... | collective-permute-start | bytes 98312 | tf_op jit(solution)/shard_map/ppermute | solution.py:12
where the time goes:
time: 249 us; the launch traced here: 247 us
  blocking collectives  122 us (49%)
  local copies, waits for them, and re-layouts  53.4 us (21%)
  starting transfers between devices  38.1 us (15%)
  other arithmetic  15.4 us (6%)
  waiting for transfers between devices  10.3 us (4%)
  between operations  7.93 us (3%)
    psum x1, blocking collectives, body(): sums = lax.psum(sums, ('rows', 'dates'))  103 us
    unnamed x68, local copies, waits for them, and re-layouts  31.8 us
    ppermute x9, starting transfers between devices, shifted(): lax.ppermute(value, axis, [(i, i + steps) for i in range(first, last)])  27.1 us
    all_to_all x1, blocking collectives, body(): out = lax.all_to_all(out, 'dates', split_axis=1, concat_axis=3, tiled=True)  18.4 us
    all_to_all x1, starting transfers between devices, body(): lax.all_to_all(both, 'dates', split_axis=3, concat_axis=1, tiled=True)  11 us
    all_to_all x2, local copies, waits for them, and re-layouts, body(): lax.all_to_all(both, 'dates', split_axis=3, concat_axis=1, tiled=True)  10.6 us
    all_to_all x1, waiting for transfers between devices, body(): lax.all_to_all(both, 'dates', split_axis=3, concat_axis=1, tiled=True)  9.63 us
    another operation x1, local copies, waits for them, and re-layouts, body(): both = jnp.stack([weight, weight * observed])  8.2 us
  transfers between devices with their start and end apart: 10, of which 2 were waited for; matrix products, arithmetic and copies ran while one was open for 2% of the time, Pallas kernels for 0%

commit v1 on v0

v1 whole, which is shorter than its diff:
```python
import functools
import jax
import jax.numpy as jnp
from jax import lax
from jax.experimental import pallas as pl
from jax.experimental.pallas import tpu as pltpu
from jax.sharding import PartitionSpec as P

MASS = 0.1
LANES = 128
UNROLL = 4
MESH = pl.DeviceIdType.MESH
RHS, WEIGHT, PRECOND, MAPPED, RESIDUAL = range(5)


def kernel(
    rows, groups, low_size,
    mask_hbm, prec_hbm, obs_hbm, edge_hbm, tau_ref, inv_hbm,
    sol_ref, res_ref,
    mask, prec, obs, edge, inv,
    weight_date, rhs_date, precond_date, mapped_date, residual_date,
    weight, rhs, precond, image, mapped, second_image, residual,
    across, across_prev, downward, downward_prev,
    down_send, up_send, from_above, from_below,
    right_send, left_send, from_left, from_right,
    part, parts,
    local_sem, send_sem, recv_sem, halo_send_sem, halo_recv_sem, sum_send_sem, sum_recv_sem,
):
    dates_here, height, columns = mask.shape
    dates, _, width = rhs.shape
    row = lax.axis_index("rows")
    group = lax.axis_index("dates")
    low, high = row % low_size, row // low_size
    high_size = rows // low_size
    above_row, below_row = (row + rows - 1) % rows, (row + 1) % rows
    left_group, right_group = (group + groups - 1) % groups, (group + 1) % groups
    my_columns = pl.ds(pl.multiple_of(group * width, width), width)

    def sum_peer(phase, step):
        if phase == 0:
            return (row, (group + step) % groups)
        if phase == 1:
            return (high * low_size + (low + step) % low_size, group)
        return (((high + step) % high_size) * low_size + low, group)

    phases = ((groups, group), (low_size, low), (high_size, high))

    barrier = pltpu.get_barrier_semaphore()
    greeted = 0
    for phase, (size, _) in enumerate(phases):
        for step in range(1, size):
            pl.semaphore_signal(
                barrier, inc=1, device_id=sum_peer(phase, step), device_id_type=MESH
            )
            greeted += 1
    for neighbour in (above_row, below_row):
        pl.semaphore_signal(barrier, inc=1, device_id=(neighbour, group), device_id_type=MESH)
        greeted += 1

    loads = [
        pltpu.make_async_copy(source, target, local_sem.at[number])
        for number, (source, target) in enumerate(
            ((mask_hbm, mask), (prec_hbm, prec), (obs_hbm, obs), (edge_hbm, edge), (inv_hbm, inv))
        )
    ]
    for load in loads:
        load.start()

    for load in loads[:3]:
        load.wait()
    for date in range(dates_here):
        here = mask[date].astype(jnp.float32) * prec[date]
        weight_date[date] = here
        rhs_date[date] = here * obs[date]
    for date in range(dates_here):
        rhs[group * dates_here + date] = rhs_date[date, :, my_columns]
        weight[group * dates_here + date] = weight_date[date, :, my_columns]
    pl.semaphore_wait(barrier, greeted)

    def inward(field, source, target, step):
        peer = (group + step) % groups
        came_from = (group + groups - step) % groups
        block = source.at[:, :, pl.ds(pl.multiple_of(peer * width, width), width)]
        sent = pltpu.make_async_remote_copy(
            block, target.at[pl.ds(group * dates_here, dates_here)],
            send_sem.at[field, peer], recv_sem.at[field, group], (row, peer), MESH,
        )
        got = pltpu.make_async_remote_copy(
            block, target.at[pl.ds(came_from * dates_here, dates_here)],
            send_sem.at[field, peer], recv_sem.at[field, came_from], (row, peer), MESH,
        )
        return sent, got

    def outward(field, source, first, target, step):
        peer = (group + step) % groups
        came_from = (group + groups - step) % groups
        block = source.at[pl.ds(first + peer * dates_here, dates_here)]
        sent = pltpu.make_async_remote_copy(
            block, target.at[:, :, my_columns],
            send_sem.at[field, peer], recv_sem.at[field, group], (row, peer), MESH,
        )
        got = pltpu.make_async_remote_copy(
            block, target.at[:, :, pl.ds(pl.multiple_of(came_from * width, width), width)],
            send_sem.at[field, peer], recv_sem.at[field, came_from], (row, peer), MESH,
        )
        return sent, got

    half = groups // 2
    steps = sorted(range(1, groups), key=lambda step: (-min(step, groups - step), step))
    assert half >= 1
    rhs_copies = [inward(RHS, rhs_date, rhs, step) for step in steps]
    weight_copies = [inward(WEIGHT, weight_date, weight, step) for step in steps]
    for sent, _ in rhs_copies:
        sent.start()
    for sent, _ in weight_copies:
        sent.start()

    loads[3].wait()
    lane = lax.broadcasted_iota(jnp.int32, (height, LANES), 1)
    col = lax.broadcasted_iota(jnp.int32, (height, width), 1)
    line = lax.broadcasted_iota(jnp.int32, (height, width), 0)
    steps_across = 0.25 * (edge[0, :, my_columns].astype(jnp.float32) + 1.0)
    steps_down = 0.25 * (edge[1, :, my_columns].astype(jnp.float32) + 1.0)
    across[...] = jnp.where((col == width - 1) & (group == groups - 1), 0.0, steps_across)
    before = (left_group + 1) * width - LANES
    edge_before = edge[0, :, pl.ds(pl.multiple_of(before, LANES), LANES)].astype(jnp.float32)
    edge_before = pltpu.roll(0.25 * (edge_before + 1.0), 1, 1)
    edge_before = jnp.where(group == 0, 0.0, edge_before)

    def with_first(block, tile):
        first = jnp.where(lane == 0, tile, block[:, :LANES])
        if width == LANES:
            return first
        return jnp.concatenate([first, block[:, LANES:]], axis=1)

    def with_last(block, tile):
        last = jnp.where(lane == LANES - 1, tile, block[:, width - LANES :])
        if width == LANES:
            return last
        return jnp.concatenate([block[:, : width - LANES], last], axis=1)

    across_prev[...] = with_first(pltpu.roll(steps_across, 1, 1), edge_before)
    down_here = jnp.where((line == height - 1) & (row == rows - 1), 0.0, steps_down)
    downward[...] = down_here
    down_send[0, dates:, :] = jnp.broadcast_to(
        down_here[height - 1 :, :], (down_send.shape[1] - dates, width)
    )
    down_send[1, dates:, :] = jnp.zeros((down_send.shape[1] - dates, width), jnp.float32)
    for field in (precond, mapped):
        field[0] = jnp.zeros((height, width), jnp.float32)
        field[dates + 1] = jnp.zeros((height, width), jnp.float32)

    def folded(block):
        total = block[:, :LANES]
        for start in range(LANES, width, LANES):
            total = total + block[:, start : start + LANES]
        return total

    def over_dates(step_of, init):
        def several(index, carry):
            for inner in range(UNROLL):
                carry = step_of(index * UNROLL + inner, carry)
            return carry

        return lax.fori_loop(0, dates // UNROLL, several, init)

    none = jnp.zeros((height, LANES), jnp.float32)

    def precondition(source, target, turn):
        def one(date, carry):
            total, to_right, to_left = carry
            out = inv[date, 0].astype(jnp.float32) * source[0]
            for other in range(1, dates):
                out = out + inv[date, other].astype(jnp.float32) * source[other]
            target[date + 1] = out
            down_send[turn, pl.ds(date, 1), :] = out[height - 1 :, :]
            up_send[turn, pl.ds(date, 1), :] = out[:1, :]
            to_right = jnp.where(
                lane == date, pltpu.roll(out[:, width - LANES :], date + 1, 1), to_right
            )
            to_left = jnp.where(lane == date, pltpu.roll(out[:, :LANES], date, 1), to_left)
            return total + folded(source[date] * out), to_right, to_left

        total, to_right, to_left = over_dates(one, (none, none, none))
        right_send[turn] = to_right
        left_send[turn] = to_left
        return total

    def halo(turn):
        pairs = (
            (down_send, from_above, (below_row, group)),
            (up_send, from_below, (above_row, group)),
            (right_send, from_left, (row, right_group)),
            (left_send, from_right, (row, left_group)),
        )
        return [
            pltpu.make_async_remote_copy(
                source.at[turn], target.at[turn],
                halo_send_sem.at[turn, number], halo_recv_sem.at[turn, number], device, MESH,
            )
            for number, (source, target, device) in enumerate(pairs)
        ]

    def operator(field, target, turn):
        def one(date, total):
            here = field[date + 1]
            above = jnp.where(
                line == 0, from_above[turn, pl.ds(date, 1), :], pltpu.roll(here, 1, 0)
            )
            below = jnp.where(
                line == height - 1,
                from_below[turn, pl.ds(date, 1), :],
                pltpu.roll(here, height - 1, 0),
            )
            left = with_first(
                pltpu.roll(here, 1, 1),
                pltpu.roll(from_left[turn], (LANES - date) % LANES, 1),
            )
            right = with_last(
                pltpu.roll(here, width - 1, 1),
                pltpu.roll(from_right[turn], LANES - 1 - date, 1),
            )
            out = (MASS + weight[date]) * here
            out = out + across[...] * (here - right) + across_prev[...] * (here - left)
            out = out + downward[...] * (here - below) + downward_prev[...] * (here - above)
            out = out + tau_ref[date + 1] * (here - field[date + 2])
            out = out + tau_ref[date] * (here - field[date])
            target[date] = out
            return total + folded(here * out)

        return over_dates(one, none)

    def bring_back(field, source, target):
        copies = [outward(field, source, 1, target, step) for step in steps]
        for sent, _ in copies:
            sent.start()
        for date in range(dates_here):
            target[date, :, my_columns] = source[1 + group * dates_here + date]
        return copies

    loads[4].wait()
    for _, got in rhs_copies:
        got.wait_recv()
    sum_rz = precondition(rhs, precond, 0)
    first_halo = halo(0)
    for copy in first_halo:
        copy.start()
    precond_copies = bring_back(PRECOND, precond, precond_date)
    for _, got in weight_copies:
        got.wait_recv()
    for copy in first_halo:
        copy.wait_recv()
    downward_prev[...] = jnp.where(
        line == 0,
        jnp.where(row == 0, 0.0, from_above[0, dates : dates + 1, :]),
        pltpu.roll(downward[...], 1, 0),
    )
    sum_d = operator(precond, image, 0)
    sum_e = precondition(image, mapped, 1)
    second_halo = halo(1)
    for copy in second_halo:
        copy.start()
    mapped_copies = bring_back(MAPPED, mapped, mapped_date)
    for copy in second_halo:
        copy.wait_recv()
    sum_f = operator(mapped, second_image, 1)

    tile_line = lax.broadcasted_iota(jnp.int32, (height, LANES), 0)
    tile = jnp.zeros((height, LANES), jnp.float32)
    for number, total in enumerate((sum_rz, sum_d, sum_e, sum_f)):
        tile = jnp.where(tile_line == number, jnp.sum(total, axis=0, keepdims=True), tile)
    sum_copies = []
    for phase, (size, mine) in enumerate(phases):
        part[phase] = tile
        parts[phase, mine] = tile
        received = []
        for step in range(1, size):
            came_from = (mine + size - step) % size
            sent = pltpu.make_async_remote_copy(
                part.at[phase], parts.at[phase, mine],
                sum_send_sem.at[phase, step], sum_recv_sem.at[phase, mine],
                sum_peer(phase, step), MESH,
            )
            sent.start()
            sum_copies.append(sent)
            received.append(
                pltpu.make_async_remote_copy(
                    part.at[phase], parts.at[phase, came_from],
                    sum_send_sem.at[phase, step], sum_recv_sem.at[phase, came_from],
                    sum_peer(phase, step), MESH,
                )
            )
        for got in received:
            got.wait_recv()
        tile = parts[phase, 0]
        for other in range(1, size):
            tile = tile + parts[phase, other]
    lines = jnp.sum(tile, axis=1, keepdims=True)
    rz, dd, ee, ff = (lines[number : number + 1] for number in range(4))
    alpha = rz / dd
    grown = alpha * ee / dd
    alpha_next = (alpha * alpha * ee - rz) / (alpha * alpha * (ff - ee * ee / dd))
    first = alpha + alpha_next * grown
    second = alpha_next * alpha
    first = jnp.broadcast_to(first, (height, width))
    second = jnp.broadcast_to(second, (height, width))

    def finish(date, carry):
        residual[date + 1] = rhs[date] - first * image[date] + second * second_image[date]
        return carry

    over_dates(finish, 0)
    residual_copies = bring_back(RESIDUAL, residual, residual_date)
    for copies in (precond_copies, mapped_copies):
        for _, got in copies:
            got.wait_recv()
    for date in range(dates_here):
        for number in range(groups):
            part_of = slice(number * width, (number + 1) * width)
            sol_ref[date, :, part_of] = (
                first * precond_date[date, :, part_of] - second * mapped_date[date, :, part_of]
            )
    for _, got in residual_copies:
        got.wait_recv()
    res_ref[...] = residual_date[...]
    for copies in (rhs_copies, weight_copies, precond_copies, mapped_copies, residual_copies):
        for sent, _ in copies:
            sent.wait_send()
    for copy in first_halo + second_halo + sum_copies:
        copy.wait_send()


def body(obs_mask, precision, observed, edge_class, temporal_weight, inverse):
    rows, groups = lax.axis_size("rows"), lax.axis_size("dates")
    low_size = 8 if rows >= 64 else 2
    dates, _, height, width = inverse.shape
    zero_one = jnp.zeros((1,), jnp.float32)
    tau = jnp.concatenate([zero_one, temporal_weight, zero_one])
    f32 = jnp.float32
    whole = observed.shape
    block = (dates, height, width)
    padded = (dates + 2, height, width)
    most = max(groups, low_size, rows // low_size)
    vmem = pltpu.VMEM
    dma = pltpu.SemaphoreType.DMA
    scratch = (
        [vmem(whole, jnp.int32), vmem(whole, f32), vmem(whole, f32)]
        + [vmem(edge_class.shape, jnp.int32), vmem(inverse.shape, jnp.bfloat16)]
        + [vmem(whole, f32)] * 5
        + [vmem(block, f32), vmem(block, f32), vmem(padded, f32), vmem(block, f32)]
        + [vmem(padded, f32), vmem(block, f32), vmem(padded, f32)]
        + [vmem((height, width), f32)] * 4
        + [vmem((2, dates + 8, width), f32), vmem((2, dates, width), f32)] * 2
        + [vmem((2, height, LANES), f32)] * 4
        + [vmem((3, height, LANES), f32), vmem((3, most, height, LANES), f32)]
        + [dma((5,)), dma((5, groups)), dma((5, groups)), dma((2, 4)), dma((2, 4))]
        + [dma((3, most)), dma((3, most))]
    )
    anywhere = pl.BlockSpec(memory_space=pl.ANY)
    return pl.pallas_call(
        functools.partial(kernel, rows, groups, low_size),
        out_shape=[jax.ShapeDtypeStruct(whole, f32)] * 2,
        in_specs=[anywhere] * 4 + [pl.BlockSpec(memory_space=pltpu.SMEM), anywhere],
        out_specs=[pl.BlockSpec(memory_space=pltpu.VMEM)] * 2,
        scratch_shapes=scratch,
        compiler_params=pltpu.CompilerParams(collective_id=0, has_side_effects=True),
        name="cg",
    )(obs_mask, precision, observed, edge_class, tau, inverse)


def solution(mesh):
    return jax.shard_map(
        body,
        mesh=mesh,
        in_specs=(
            P("dates", "rows", None),
            P("dates", "rows", None),
            P("dates", "rows", None),
            P(None, "rows", None),
            P(),
            P(None, None, "rows", "dates"),
        ),
        out_specs=(P("dates", "rows", None), P("dates", "rows", None)),
        check_vma=False,
    )
```

time: 249 us -> 66 us (0.27)
  blocking collectives: 122 us -> 0 us
  Pallas kernels: 0 us -> 60.6 us
  local copies, waits for them, and re-layouts: 53.4 us -> 3.34 us
  starting transfers between devices: 38.1 us -> 0 us
  other arithmetic: 15.4 us -> 1.24 us
  waiting for transfers between devices: 10.3 us -> 0 us
  between operations: 7.93 us -> 0.64 us
    psum x1 -> x0, blocking collectives: 103 us -> none  [body(): sums = lax.psum(sums, ('rows', 'dates'))]
    pallas_call x0 -> x1, Pallas kernels: none -> 60.6 us  [body(): pl.pallas_call(functools.partial(kernel, rows, groups, low_size), out_sha...]
    unnamed x68 -> x2, local copies, waits for them, and re-layouts: 31.8 us -> 3.34 us
    ppermute x9 -> x0, starting transfers between devices: 27.1 us -> none  [shifted(): lax.ppermute(value, axis, [(i, i + steps) for i in range(first, last)])]
    all_to_all x1 -> x0, blocking collectives: 18.4 us -> none  [body(): out = lax.all_to_all(out, 'dates', split_axis=1, concat_axis=3, tiled=True)]
    all_to_all x1 -> x0, starting transfers between devices: 11 us -> none  [body(): lax.all_to_all(both, 'dates', split_axis=3, concat_axis=1, tiled=True)]
    all_to_all x2 -> x0, local copies, waits for them, and re-layouts: 10.6 us -> none  [body(): lax.all_to_all(both, 'dates', split_axis=3, concat_axis=1, tiled=True)]
    all_to_all x1 -> x0, waiting for transfers between devices: 9.63 us -> none  [body(): lax.all_to_all(both, 'dates', split_axis=3, concat_axis=1, tiled=True)]
  transfers between devices with their start and end apart: 10 -> 0, of which waited for: 2 -> 0; matrix products, arithmetic and copies ran while one was open for 2% -> 0% of each run, Pallas kernels for 0% -> 0%
where the time goes in v1:
time: 66 us; the launch traced here: 65.8 us
  Pallas kernels  60.6 us (92%)
  local copies, waits for them, and re-layouts  3.34 us (5%)
  other arithmetic  1.24 us (2%)
    pallas_call x1, Pallas kernels, body(): pl.pallas_call(functools.partial(kernel, rows, groups, low_size), out_sha...  60.6 us
    unnamed x2, local copies, waits for them, and re-layouts  3.34 us

profile of v1, /device:TPU:1, one launch (start us, length us, event | category | flops | bytes accessed | tf_op | source)
XLA Modules:
  0.0 65.8 jit_solution(11350022962831096055)
XLA Ops:
  0.6 1.2 %pad_maximum_fusion.tau_ref = f32[17]{0:T(128)} fusion(f32[1]{0:T(128)} %constant.0.clone.1, f32[15]{0:T(128)} %param.10), kind=kLoop, calls=%fused_computation | loop fusion | flops 34 | bytes 132 | tf_op jit(solution)/shard_map/concatenate | solution.py:338
  1.9 60.6 %cg.1 = (f32[2,8,4096]{2,1,0:T(8,128)}, f32[2,8,4096]{2,1,0:T(8,128)}) custom-call(s32[2,8,4096]{2,1,0:T(8,128)} %mask_hbm.1, f32[2,8,4096]{2,1,0:T(8,128)} %prec_hbm.1, f32[2,8,4096]{2,1,0:T(8,128)} %obs_hbm.1, s32[2,8,4096]{2,1,0:T(8,128)} %edge_hbm.1, f32[17]{0:T(128)} %pad_maximum_fusion.tau_ref, bf16[16,16,8,512]{3,2,1,0:T(8,128)(2,1)} %inv_hbm.1), custom_call_target="tpu_custom_call" | custom-call | tf_op jit(solution)/shard_map/cg/pallas_call | solution.py:360
  62.5 1.7 %copy.10 = f32[2,8,4096]{2,1,0:T(8,128)} copy(f32[2,8,4096]{2,1,0:T(8,128)} %get-tuple-element.4) | data formatting | bytes 524288
  64.2 1.7 %copy.11 = f32[2,8,4096]{2,1,0:T(8,128)} copy(f32[2,8,4096]{2,1,0:T(8,128)} %get-tuple-element.5) | data formatting | bytes 524288

commit v2 on v1

--- a/solution.py
+++ b/solution.py
@@ -9,8 +9,9 @@
 MASS = 0.1
 LANES = 128
 UNROLL = 4
+VMEM_BYTES = 16 * 1024 * 1024
 MESH = pl.DeviceIdType.MESH
-RHS, WEIGHT, PRECOND, MAPPED, RESIDUAL = range(5)
+RHS, WEIGHT, PRECOND, IMAGE, MAPPED, SECOND = range(6)
 
 
 def kernel(
@@ -18,8 +19,8 @@
     mask_hbm, prec_hbm, obs_hbm, edge_hbm, tau_ref, inv_hbm,
     sol_ref, res_ref,
     mask, prec, obs, edge, inv,
-    weight_date, rhs_date, precond_date, mapped_date, residual_date,
-    weight, rhs, precond, image, mapped, second_image, residual,
+    weight_date, rhs_date, precond_date, image_date, mapped_date, second_date,
+    weight, rhs, precond, image, mapped, second_image,
     across, across_prev, downward, downward_prev,
     down_send, up_send, from_above, from_below,
     right_send, left_send, from_left, from_right,
@@ -38,12 +39,12 @@
 
     def sum_peer(phase, step):
         if phase == 0:
-            return (row, (group + step) % groups)
+            return (high * low_size + (low + step) % low_size, group)
         if phase == 1:
-            return (high * low_size + (low + step) % low_size, group)
-        return (((high + step) % high_size) * low_size + low, group)
-
-    phases = ((groups, group), (low_size, low), (high_size, high))
+            return (((high + step) % high_size) * low_size + low, group)
+        return (row, (group + step) % groups)
+
+    phases = ((low_size, low), (high_size, high), (groups, group))
 
     barrier = pltpu.get_barrier_semaphore()
     greeted = 0
@@ -220,22 +221,24 @@
                 pltpu.roll(here, width - 1, 1),
                 pltpu.roll(from_right[turn], LANES - 1 - date, 1),
             )
+            tau_up = jnp.where(date < dates - 1, tau_ref[jnp.minimum(date, dates - 2)], 0.0)
+            tau_down = jnp.where(date > 0, tau_ref[jnp.maximum(date - 1, 0)], 0.0)
             out = (MASS + weight[date]) * here
             out = out + across[...] * (here - right) + across_prev[...] * (here - left)
             out = out + downward[...] * (here - below) + downward_prev[...] * (here - above)
-            out = out + tau_ref[date + 1] * (here - field[date + 2])
-            out = out + tau_ref[date] * (here - field[date])
+            out = out + tau_up * (here - field[date + 2])
+            out = out + tau_down * (here - field[date])
             target[date] = out
             return total + folded(here * out)
 
         return over_dates(one, none)
 
-    def bring_back(field, source, target):
-        copies = [outward(field, source, 1, target, step) for step in steps]
+    def bring_back(field, source, first, target):
+        copies = [outward(field, source, first, target, step) for step in steps]
         for sent, _ in copies:
             sent.start()
         for date in range(dates_here):
-            target[date, :, my_columns] = source[1 + group * dates_here + date]
+            target[date, :, my_columns] = source[first + group * dates_here + date]
         return copies
 
     loads[4].wait()
@@ -245,7 +248,7 @@
     first_halo = halo(0)
     for copy in first_halo:
         copy.start()
-    precond_copies = bring_back(PRECOND, precond, precond_date)
+    precond_copies = bring_back(PRECOND, precond, 1, precond_date)
     for _, got in weight_copies:
         got.wait_recv()
     for copy in first_halo:
@@ -256,14 +259,16 @@
         pltpu.roll(downward[...], 1, 0),
     )
     sum_d = operator(precond, image, 0)
+    image_copies = bring_back(IMAGE, image, 0, image_date)
     sum_e = precondition(image, mapped, 1)
     second_halo = halo(1)
     for copy in second_halo:
         copy.start()
-    mapped_copies = bring_back(MAPPED, mapped, mapped_date)
+    mapped_copies = bring_back(MAPPED, mapped, 1, mapped_date)
     for copy in second_halo:
         copy.wait_recv()
     sum_f = operator(mapped, second_image, 1)
+    second_copies = bring_back(SECOND, second_image, 0, second_date)
 
     tile_line = lax.broadcasted_iota(jnp.int32, (height, LANES), 0)
     tile = jnp.zeros((height, LANES), jnp.float32)
@@ -305,25 +310,28 @@
     first = jnp.broadcast_to(first, (height, width))
     second = jnp.broadcast_to(second, (height, width))
 
-    def finish(date, carry):
-        residual[date + 1] = rhs[date] - first * image[date] + second * second_image[date]
-        return carry
-
-    over_dates(finish, 0)
-    residual_copies = bring_back(RESIDUAL, residual, residual_date)
-    for copies in (precond_copies, mapped_copies):
-        for _, got in copies:
-            got.wait_recv()
-    for date in range(dates_here):
-        for number in range(groups):
-            part_of = slice(number * width, (number + 1) * width)
-            sol_ref[date, :, part_of] = (
-                first * precond_date[date, :, part_of] - second * mapped_date[date, :, part_of]
-            )
-    for _, got in residual_copies:
-        got.wait_recv()
-    res_ref[...] = residual_date[...]
-    for copies in (rhs_copies, weight_copies, precond_copies, mapped_copies, residual_copies):
+    def whole_row(output, combine, *copied):
+        for copies in copied:
+            for _, got in copies:
+                got.wait_recv()
+        for date in range(dates_here):
+            for number in range(groups):
+                output[date, :, number * width : (number + 1) * width] = combine(
+                    (date, slice(None), slice(number * width, (number + 1) * width))
+                )
+
+    whole_row(
+        sol_ref,
+        lambda at: first * precond_date[at] - second * mapped_date[at],
+        precond_copies, mapped_copies,
+    )
+    whole_row(
+        res_ref,
+        lambda at: rhs_date[at] - first * image_date[at] + second * second_date[at],
+        image_copies, second_copies,
+    )
+    back = (precond_copies, image_copies, mapped_copies, second_copies)
+    for copies in (rhs_copies, weight_copies) + back:
         for sent, _ in copies:
             sent.wait_send()
     for copy in first_halo + second_halo + sum_copies:
@@ -334,8 +342,6 @@
     rows, groups = lax.axis_size("rows"), lax.axis_size("dates")
     low_size = 8 if rows >= 64 else 2
     dates, _, height, width = inverse.shape
-    zero_one = jnp.zeros((1,), jnp.float32)
-    tau = jnp.concatenate([zero_one, temporal_weight, zero_one])
     f32 = jnp.float32
     whole = observed.shape
     block = (dates, height, width)
@@ -346,26 +352,26 @@
     scratch = (
         [vmem(whole, jnp.int32), vmem(whole, f32), vmem(whole, f32)]
         + [vmem(edge_class.shape, jnp.int32), vmem(inverse.shape, jnp.bfloat16)]
-        + [vmem(whole, f32)] * 5
+        + [vmem(whole, f32)] * 6
         + [vmem(block, f32), vmem(block, f32), vmem(padded, f32), vmem(block, f32)]
-        + [vmem(padded, f32), vmem(block, f32), vmem(padded, f32)]
+        + [vmem(padded, f32), vmem(block, f32)]
         + [vmem((height, width), f32)] * 4
         + [vmem((2, dates + 8, width), f32), vmem((2, dates, width), f32)] * 2
         + [vmem((2, height, LANES), f32)] * 4
         + [vmem((3, height, LANES), f32), vmem((3, most, height, LANES), f32)]
-        + [dma((5,)), dma((5, groups)), dma((5, groups)), dma((2, 4)), dma((2, 4))]
+        + [dma((5,)), dma((6, groups)), dma((6, groups)), dma((2, 4)), dma((2, 4))]
         + [dma((3, most)), dma((3, most))]
     )
-    anywhere = pl.BlockSpec(memory_space=pl.ANY)
+    anywhere = pl.BlockSpec(memory_space=pltpu.HBM)
     return pl.pallas_call(
         functools.partial(kernel, rows, groups, low_size),
         out_shape=[jax.ShapeDtypeStruct(whole, f32)] * 2,
         in_specs=[anywhere] * 4 + [pl.BlockSpec(memory_space=pltpu.SMEM), anywhere],
         out_specs=[pl.BlockSpec(memory_space=pltpu.VMEM)] * 2,
         scratch_shapes=scratch,
-        compiler_params=pltpu.CompilerParams(collective_id=0, has_side_effects=True),
+        compiler_params=pltpu.CompilerParams(collective_id=0, has_side_effects=True, vmem_limit_bytes=VMEM_BYTES),
         name="cg",
-    )(obs_mask, precision, observed, edge_class, tau, inverse)
+    )(obs_mask, precision, observed, edge_class, temporal_weight, inverse)
 
 
 def solution(mesh):

time: 66 us -> 65 us (0.985)
  local copies, waits for them, and re-layouts: 3.34 us -> 7.44 us
  Pallas kernels: 60.6 us -> 56.6 us
  other arithmetic: 1.24 us -> 0 us
    unnamed x2 -> x14, local copies, waits for them, and re-layouts: 3.34 us -> 7.44 us
    pallas_call x1, Pallas kernels: 60.6 us -> 56.6 us  [body(): pl.pallas_call(functools.partial(kernel, rows, groups, low_size), out_sha...]
    concatenate x1 -> x0, other arithmetic: 1.24 us -> none  [body(): tau = jnp.concatenate([zero_one, temporal_weight, zero_one])]
where the time goes in v2:
time: 65 us; the launch traced here: 64.7 us
  Pallas kernels  56.6 us (87%)
  local copies, waits for them, and re-layouts  7.44 us (11%)
  between operations  0.65 us (1%)
    pallas_call x1, Pallas kernels, body(): pl.pallas_call(functools.partial(kernel, rows, groups, low_size), out_sha...  56.6 us
    unnamed x14, local copies, waits for them, and re-layouts  7.44 us

profile of v2, /device:TPU:1, one launch (start us, length us, event | category | flops | bytes accessed | tf_op | source)
XLA Modules:
  0.0 64.7 jit_solution(7958266551150759517)
XLA Ops:
  0.6 0.0 copy-start
  0.6 1.6 %copy-done = bf16[16,16,8,512]{3,2,1,0:T(8,128)(2,1)S(1)} copy-done((bf16[16,16,8,512]{3,2,1,0:T(8,128)(2,1)S(1)}, bf16[16,16,8,512]{3,2,1,0:T(8,128)(2,1)}, u32[]{:S(2)}) %copy-start) | copy-done | bytes 2097176
  2.2 0.0 copy-start.1
  2.2 0.9 %copy-done.1 = s32[2,8,4096]{2,1,0:T(8,128)S(1)} copy-done((s32[2,8,4096]{2,1,0:T(8,128)S(1)}, s32[2,8,4096]{2,1,0:T(8,128)}, u32[]{:S(2)}) %copy-start.1) | copy-done | bytes 262168
  3.2 0.0 copy-start.2
  3.2 0.9 %copy-done.2 = f32[2,8,4096]{2,1,0:T(8,128)S(1)} copy-done((f32[2,8,4096]{2,1,0:T(8,128)S(1)}, f32[2,8,4096]{2,1,0:T(8,128)}, u32[]{:S(2)}) %copy-start.2) | copy-done | bytes 262168
  4.1 0.0 copy-start.3
  4.1 0.9 %copy-done.3 = f32[2,8,4096]{2,1,0:T(8,128)S(1)} copy-done((f32[2,8,4096]{2,1,0:T(8,128)S(1)}, f32[2,8,4096]{2,1,0:T(8,128)}, u32[]{:S(2)}) %copy-start.3) | copy-done | bytes 262168
  5.1 0.0 copy-start.4
  5.1 0.9 %copy-done.4 = s32[2,8,4096]{2,1,0:T(8,128)S(1)} copy-done((s32[2,8,4096]{2,1,0:T(8,128)S(1)}, s32[2,8,4096]{2,1,0:T(8,128)}, u32[]{:S(2)}) %copy-start.4) | copy-done | bytes 262168
  6.0 0.0 copy-start.5
  6.0 0.7 %copy-done.5 = f32[15]{0:T(128)S(1)} copy-done((f32[15]{0:T(128)S(1)}, f32[15]{0:T(128)}, u32[]{:S(2)}) %copy-start.5) | copy-done | bytes 84
  6.7 56.6 %cg.1 = (f32[2,8,4096]{2,1,0:T(8,128)S(1)}, f32[2,8,4096]{2,1,0:T(8,128)S(1)}) custom-call(s32[2,8,4096]{2,1,0:T(8,128)S(1)} %copy-done.1, f32[2,8,4096]{2,1,0:T(8,128)S(1)} %copy-done.2, f32[2,8,4096]{2,1,0:T(8,128)S(1)} %copy-done.3, s32[2,8,4096]{2,1,0:T(8,128)S(1)} %copy-done.4, f32[15]{0:T(128)S(1)} %copy-done.5, bf16[16,16,8,512]{3,2,1,0:T(8,128)(2,1)S(1)} %copy-done), custom_call_target="tpu_custom_call" | custom-call | tf_op jit(solution)/shard_map/cg/pallas_call | solution.py:366
  63.3 0.7 %copy.10 = f32[2,8,4096]{2,1,0:T(8,128)} copy(f32[2,8,4096]{2,1,0:T(8,128)S(1)} %get-tuple-element.4) | data formatting | bytes 524288
  64.0 0.7 %copy.11 = f32[2,8,4096]{2,1,0:T(8,128)} copy(f32[2,8,4096]{2,1,0:T(8,128)S(1)} %get-tuple-element.5) | data formatting | bytes 524288
Async XLA Ops:
  0.6 1.6 %copy-start = (bf16[16,16,8,512]{3,2,1,0:T(8,128)(2,1)S(1)}, bf16[16,16,8,512]{3,2,1,0:T(8,128)(2,1)}, u32[]{:S(2)}) copy-start(bf16[16,16,8,512]{3,2,1,0:T(8,128)(2,1)} %inv_hbm.1) | copy-start | bytes 6291460
  2.2 0.9 %copy-start.1 = (s32[2,8,4096]{2,1,0:T(8,128)S(1)}, s32[2,8,4096]{2,1,0:T(8,128)}, u32[]{:S(2)}) copy-start(s32[2,8,4096]{2,1,0:T(8,128)} %mask_hbm.1) | copy-start | bytes 786436
  3.2 0.9 %copy-start.2 = (f32[2,8,4096]{2,1,0:T(8,128)S(1)}, f32[2,8,4096]{2,1,0:T(8,128)}, u32[]{:S(2)}) copy-start(f32[2,8,4096]{2,1,0:T(8,128)} %prec_hbm.1) | copy-start | bytes 786436
  4.1 0.9 %copy-start.3 = (f32[2,8,4096]{2,1,0:T(8,128)S(1)}, f32[2,8,4096]{2,1,0:T(8,128)}, u32[]{:S(2)}) copy-start(f32[2,8,4096]{2,1,0:T(8,128)} %obs_hbm.1) | copy-start | bytes 786436
  5.1 0.9 %copy-start.4 = (s32[2,8,4096]{2,1,0:T(8,128)S(1)}, s32[2,8,4096]{2,1,0:T(8,128)}, u32[]{:S(2)}) copy-start(s32[2,8,4096]{2,1,0:T(8,128)} %edge_hbm.1) | copy-start | bytes 786436
  6.0 0.7 %copy-start.5 = (f32[15]{0:T(128)S(1)}, f32[15]{0:T(128)}, u32[]{:S(2)}) copy-start(f32[15]{0:T(128)} %tau_ref.1) | copy-start | bytes 184

commit v3 on v2

--- a/solution.py
+++ b/solution.py
@@ -16,7 +16,7 @@
 
 def kernel(
     rows, groups, low_size,
-    mask_hbm, prec_hbm, obs_hbm, edge_hbm, tau_ref, inv_hbm,
+    mask_hbm, prec_hbm, obs_hbm, edge_hbm, tau_hbm, inv_hbm,
     sol_ref, res_ref,
     mask, prec, obs, edge, inv,
     weight_date, rhs_date, precond_date, image_date, mapped_date, second_date,
@@ -25,7 +25,7 @@
     down_send, up_send, from_above, from_below,
     right_send, left_send, from_left, from_right,
     part, parts,
-    local_sem, send_sem, recv_sem, halo_send_sem, halo_recv_sem, sum_send_sem, sum_recv_sem,
+    tau_ref, local_sem, send_sem, recv_sem, halo_send_sem, halo_recv_sem, sum_send_sem, sum_recv_sem,
 ):
     dates_here, height, columns = mask.shape
     dates, _, width = rhs.shape
@@ -39,12 +39,12 @@
 
     def sum_peer(phase, step):
         if phase == 0:
+            return (row, (group + step) % groups)
+        if phase == 1:
             return (high * low_size + (low + step) % low_size, group)
-        if phase == 1:
-            return (((high + step) % high_size) * low_size + low, group)
-        return (row, (group + step) % groups)
-
-    phases = ((low_size, low), (high_size, high), (groups, group))
+        return (((high + step) % high_size) * low_size + low, group)
+
+    phases = ((groups, group), (low_size, low), (high_size, high))
 
     barrier = pltpu.get_barrier_semaphore()
     greeted = 0
@@ -61,7 +61,7 @@
     loads = [
         pltpu.make_async_copy(source, target, local_sem.at[number])
         for number, (source, target) in enumerate(
-            ((mask_hbm, mask), (prec_hbm, prec), (obs_hbm, obs), (edge_hbm, edge), (inv_hbm, inv))
+            ((mask_hbm, mask), (prec_hbm, prec), (obs_hbm, obs), (edge_hbm, edge), (inv_hbm, inv), (tau_hbm, tau_ref))
         )
     ]
     for load in loads:
@@ -233,22 +233,26 @@
 
         return over_dates(one, none)
 
-    def bring_back(field, source, first, target):
-        copies = [outward(field, source, first, target, step) for step in steps]
+    def bring_back(field, source, first, target, chosen=steps):
+        copies = [outward(field, source, first, target, step) for step in chosen]
         for sent, _ in copies:
             sent.start()
+        if chosen[-1] != steps[-1]:
+            return copies
         for date in range(dates_here):
             target[date, :, my_columns] = source[first + group * dates_here + date]
         return copies
 
     loads[4].wait()
+    loads[5].wait()
     for _, got in rhs_copies:
         got.wait_recv()
     sum_rz = precondition(rhs, precond, 0)
     first_halo = halo(0)
     for copy in first_halo:
         copy.start()
-    precond_copies = bring_back(PRECOND, precond, 1, precond_date)
+    early = len(steps) // 3
+    precond_copies = bring_back(PRECOND, precond, 1, precond_date, steps[:early])
     for _, got in weight_copies:
         got.wait_recv()
     for copy in first_halo:
@@ -259,16 +263,14 @@
         pltpu.roll(downward[...], 1, 0),
     )
     sum_d = operator(precond, image, 0)
-    image_copies = bring_back(IMAGE, image, 0, image_date)
     sum_e = precondition(image, mapped, 1)
     second_halo = halo(1)
     for copy in second_halo:
         copy.start()
-    mapped_copies = bring_back(MAPPED, mapped, 1, mapped_date)
+    precond_copies += bring_back(PRECOND, precond, 1, precond_date, steps[early:])
     for copy in second_halo:
         copy.wait_recv()
     sum_f = operator(mapped, second_image, 1)
-    second_copies = bring_back(SECOND, second_image, 0, second_date)
 
     tile_line = lax.broadcasted_iota(jnp.int32, (height, LANES), 0)
     tile = jnp.zeros((height, LANES), jnp.float32)
@@ -295,6 +297,10 @@
                     sum_peer(phase, step), MESH,
                 )
             )
+        if phase == 0:
+            mapped_copies = bring_back(MAPPED, mapped, 1, mapped_date)
+            image_copies = bring_back(IMAGE, image, 0, image_date)
+            second_copies = bring_back(SECOND, second_image, 0, second_date)
         for got in received:
             got.wait_recv()
         tile = parts[phase, 0]
@@ -359,19 +365,23 @@
         + [vmem((2, dates + 8, width), f32), vmem((2, dates, width), f32)] * 2
         + [vmem((2, height, LANES), f32)] * 4
         + [vmem((3, height, LANES), f32), vmem((3, most, height, LANES), f32)]
-        + [dma((5,)), dma((6, groups)), dma((6, groups)), dma((2, 4)), dma((2, 4))]
+        + [pltpu.SMEM((dates - 1,), f32), dma((6,)), dma((6, groups)), dma((6, groups)), dma((2, 4)), dma((2, 4))]
         + [dma((3, most)), dma((3, most))]
     )
     anywhere = pl.BlockSpec(memory_space=pltpu.HBM)
+    in_hbm = [
+        pltpu.with_memory_space_constraint(array, pltpu.HBM)
+        for array in (obs_mask, precision, observed, edge_class, temporal_weight, inverse)
+    ]
     return pl.pallas_call(
         functools.partial(kernel, rows, groups, low_size),
         out_shape=[jax.ShapeDtypeStruct(whole, f32)] * 2,
-        in_specs=[anywhere] * 4 + [pl.BlockSpec(memory_space=pltpu.SMEM), anywhere],
+        in_specs=[anywhere] * 6,
         out_specs=[pl.BlockSpec(memory_space=pltpu.VMEM)] * 2,
         scratch_shapes=scratch,
         compiler_params=pltpu.CompilerParams(collective_id=0, has_side_effects=True, vmem_limit_bytes=VMEM_BYTES),
         name="cg",
-    )(obs_mask, precision, observed, edge_class, temporal_weight, inverse)
+    )(*in_hbm)
 
 
 def solution(mesh):

time: 65 us -> 56.2 us (0.86)
  local copies, waits for them, and re-layouts: 7.44 us -> 1.41 us
  Pallas kernels: 56.6 us -> 54 us
    unnamed x14 -> x2, local copies, waits for them, and re-layouts: 7.44 us -> 1.41 us
    pallas_call x1, Pallas kernels: 56.6 us -> 54 us  [body(): pl.pallas_call(functools.partial(kernel, rows, groups, low_size), out_sha...]
where the time goes in v3:
time: 56.2 us; the launch traced here: 56.1 us
  Pallas kernels  54 us (96%)
  local copies, waits for them, and re-layouts  1.41 us (3%)
  between operations  0.64 us (1%)
    pallas_call x1, Pallas kernels, body(): pl.pallas_call(functools.partial(kernel, rows, groups, low_size), out_sha...  54 us
    unnamed x2, local copies, waits for them, and re-layouts  1.41 us

profile of v3, /device:TPU:1, one launch (start us, length us, event | category | flops | bytes accessed | tf_op | source)
XLA Modules:
  0.0 56.1 jit_solution(17559642370145185930)
XLA Ops:
  0.6 54.0 %cg.1 = (f32[2,8,4096]{2,1,0:T(8,128)S(1)}, f32[2,8,4096]{2,1,0:T(8,128)S(1)}) custom-call(s32[2,8,4096]{2,1,0:T(8,128)} %mask_hbm.1, f32[2,8,4096]{2,1,0:T(8,128)} %prec_hbm.1, f32[2,8,4096]{2,1,0:T(8,128)} %obs_hbm.1, s32[2,8,4096]{2,1,0:T(8,128)} %edge_hbm.1, f32[15]{0:T(128)} %tau_hbm.1, bf16[16,16,8,512]{3,2,1,0:T(8,128)(2,1)} %inv_hbm.1), custom_call_target="tpu_custom_call" | custom-call | tf_op jit(solution)/shard_map/cg/pallas_call | solution.py:376
  54.7 0.7 %copy.10 = f32[2,8,4096]{2,1,0:T(8,128)} copy(f32[2,8,4096]{2,1,0:T(8,128)S(1)} %get-tuple-element.4) | data formatting | bytes 524288
  55.4 0.7 %copy.11 = f32[2,8,4096]{2,1,0:T(8,128)} copy(f32[2,8,4096]{2,1,0:T(8,128)S(1)} %get-tuple-element.5) | data formatting | bytes 524288

commit v4 on v3

--- a/solution.py
+++ b/solution.py
@@ -11,7 +11,7 @@
 UNROLL = 4
 VMEM_BYTES = 16 * 1024 * 1024
 MESH = pl.DeviceIdType.MESH
-RHS, WEIGHT, PRECOND, IMAGE, MAPPED, SECOND = range(6)
+RHS, WEIGHT, PRECOND, MAPPED = range(4)
 
 
 def kernel(
@@ -19,13 +19,14 @@
     mask_hbm, prec_hbm, obs_hbm, edge_hbm, tau_hbm, inv_hbm,
     sol_ref, res_ref,
     mask, prec, obs, edge, inv,
-    weight_date, rhs_date, precond_date, image_date, mapped_date, second_date,
-    weight, rhs, precond, image, mapped, second_image,
+    weight_date, rhs_date, precond_date, mapped_date,
+    weight, rhs, precond, image, mapped,
+    date_down_send, date_up_send, from_above_date, from_below_date, from_before, from_after,
     across, across_prev, downward, downward_prev,
     down_send, up_send, from_above, from_below,
     right_send, left_send, from_left, from_right,
     part, parts,
-    tau_ref, local_sem, send_sem, recv_sem, halo_send_sem, halo_recv_sem, sum_send_sem, sum_recv_sem,
+    tau_ref, local_sem, send_sem, recv_sem, halo_send_sem, halo_recv_sem, date_send_sem, date_recv_sem, sum_send_sem, sum_recv_sem,
 ):
     dates_here, height, columns = mask.shape
     dates, _, width = rhs.shape
@@ -147,6 +148,11 @@
         down_here[height - 1 :, :], (down_send.shape[1] - dates, width)
     )
     down_send[1, dates:, :] = jnp.zeros((down_send.shape[1] - dates, width), jnp.float32)
+    rest = slice(dates_here, height)
+    all_down = 0.25 * (edge[1, height - 1 :, :].astype(jnp.float32) + 1.0)
+    for turn in range(2):
+        date_down_send[turn, rest, :] = jnp.broadcast_to(all_down, (height - dates_here, columns))
+        date_up_send[turn, rest, :] = jnp.zeros((height - dates_here, columns), jnp.float32)
     for field in (precond, mapped):
         field[0] = jnp.zeros((height, width), jnp.float32)
         field[dates + 1] = jnp.zeros((height, width), jnp.float32)
@@ -228,7 +234,8 @@
             out = out + downward[...] * (here - below) + downward_prev[...] * (here - above)
             out = out + tau_up * (here - field[date + 2])
             out = out + tau_down * (here - field[date])
-            target[date] = out
+            if target is not None:
+                target[date] = out
             return total + folded(here * out)
 
         return over_dates(one, none)
@@ -270,7 +277,30 @@
     precond_copies += bring_back(PRECOND, precond, 1, precond_date, steps[early:])
     for copy in second_halo:
         copy.wait_recv()
-    sum_f = operator(mapped, second_image, 1)
+    sum_f = operator(mapped, None, 1)
+
+    def date_halo(turn, field, copies):
+        for _, got in copies:
+            got.wait_recv()
+        for date in range(dates_here):
+            date_down_send[turn, date : date + 1, :] = field[date, height - 1 :, :]
+            date_up_send[turn, date : date + 1, :] = field[date, :1, :]
+        pairs = (
+            (date_down_send.at[turn], from_above_date, (below_row, group)),
+            (date_up_send.at[turn], from_below_date, (above_row, group)),
+            (field.at[dates_here - 1], from_before, (row, right_group)),
+            (field.at[0], from_after, (row, left_group)),
+        )
+        started = [
+            pltpu.make_async_remote_copy(
+                source, target.at[turn],
+                date_send_sem.at[turn, number], date_recv_sem.at[turn, number], device, MESH,
+            )
+            for number, (source, target, device) in enumerate(pairs)
+        ]
+        for copy in started:
+            copy.start()
+        return started
 
     tile_line = lax.broadcasted_iota(jnp.int32, (height, LANES), 0)
     tile = jnp.zeros((height, LANES), jnp.float32)
@@ -299,8 +329,9 @@
             )
         if phase == 0:
             mapped_copies = bring_back(MAPPED, mapped, 1, mapped_date)
-            image_copies = bring_back(IMAGE, image, 0, image_date)
-            second_copies = bring_back(SECOND, second_image, 0, second_date)
+            precond_halo = date_halo(0, precond_date, precond_copies)
+        if phase == 2:
+            mapped_halo = date_halo(1, mapped_date, mapped_copies)
         for got in received:
             got.wait_recv()
         tile = parts[phase, 0]
@@ -316,31 +347,70 @@
     first = jnp.broadcast_to(first, (height, width))
     second = jnp.broadcast_to(second, (height, width))
 
-    def whole_row(output, combine, *copied):
-        for copies in copied:
-            for _, got in copies:
-                got.wait_recv()
+    def combined(at_precond, at_mapped):
+        return first * at_precond - second * at_mapped
+
+    spans = [slice(number * width, (number + 1) * width) for number in range(groups)]
+    for date in range(dates_here):
+        for span in spans:
+            sol_ref[date, :, span] = combined(
+                precond_date[date, :, span], mapped_date[date, :, span]
+            )
+    for copy in precond_halo + mapped_halo:
+        copy.wait_recv()
+
+    for number, span in enumerate(spans):
+        tile_before = slice(max(span.start - LANES, 0), max(span.start, LANES))
+        tile_after = slice(min(span.stop, columns - LANES), min(span.stop + LANES, columns))
+        ahead = 0.25 * (edge[0, :, span].astype(jnp.float32) + 1.0)
+        behind = 0.25 * (edge[0, :, tile_before].astype(jnp.float32) + 1.0)
+        behind = with_first(pltpu.roll(ahead, 1, 1), pltpu.roll(behind, 1, 1))
+        if number == 0:
+            behind = jnp.where(col == 0, 0.0, behind)
+        if number == groups - 1:
+            ahead = jnp.where(col == width - 1, 0.0, ahead)
+        under = 0.25 * (edge[1, :, span].astype(jnp.float32) + 1.0)
+        under = jnp.where((line == height - 1) & (row == rows - 1), 0.0, under)
+        over = jnp.where(
+            line == 0,
+            jnp.where(row == 0, 0.0, from_above_date[0, dates_here : dates_here + 1, span]),
+            pltpu.roll(under, 1, 0),
+        )
         for date in range(dates_here):
-            for number in range(groups):
-                output[date, :, number * width : (number + 1) * width] = combine(
-                    (date, slice(None), slice(number * width, (number + 1) * width))
-                )
-
-    whole_row(
-        sol_ref,
-        lambda at: first * precond_date[at] - second * mapped_date[at],
-        precond_copies, mapped_copies,
-    )
-    whole_row(
-        res_ref,
-        lambda at: rhs_date[at] - first * image_date[at] + second * second_date[at],
-        image_copies, second_copies,
-    )
-    back = (precond_copies, image_copies, mapped_copies, second_copies)
+            when = group * dates_here + date
+            tau_up = jnp.where(when < dates - 1, tau_ref[jnp.minimum(when, dates - 2)], 0.0)
+            tau_down = jnp.where(when > 0, tau_ref[jnp.maximum(when - 1, 0)], 0.0)
+            here = sol_ref[date, :, span]
+            this = slice(date, date + 1)
+            above = combined(from_above_date[0, this, span], from_above_date[1, this, span])
+            below = combined(from_below_date[0, this, span], from_below_date[1, this, span])
+            above = jnp.where(line == 0, above, pltpu.roll(here, 1, 0))
+            below = jnp.where(line == height - 1, below, pltpu.roll(here, height - 1, 0))
+            left = with_first(
+                pltpu.roll(here, 1, 1), pltpu.roll(sol_ref[date, :, tile_before], 1, 1)
+            )
+            right = with_last(
+                pltpu.roll(here, width - 1, 1),
+                pltpu.roll(sol_ref[date, :, tile_after], LANES - 1, 1),
+            )
+            if date > 0:
+                before_here = sol_ref[date - 1, :, span]
+            else:
+                before_here = combined(from_before[0, :, span], from_before[1, :, span])
+            if date + 1 < dates_here:
+                after_here = sol_ref[date + 1, :, span]
+            else:
+                after_here = combined(from_after[0, :, span], from_after[1, :, span])
+            out = (MASS + weight_date[date, :, span]) * here
+            out = out + ahead * (here - right) + behind * (here - left)
+            out = out + under * (here - below) + over * (here - above)
+            out = out + tau_up * (here - after_here) + tau_down * (here - before_here)
+            res_ref[date, :, span] = rhs_date[date, :, span] - out
+    back = (precond_copies, mapped_copies)
     for copies in (rhs_copies, weight_copies) + back:
         for sent, _ in copies:
             sent.wait_send()
-    for copy in first_halo + second_halo + sum_copies:
+    for copy in first_halo + second_halo + precond_halo + mapped_halo + sum_copies:
         copy.wait_send()
 
 
@@ -358,14 +428,15 @@
     scratch = (
         [vmem(whole, jnp.int32), vmem(whole, f32), vmem(whole, f32)]
         + [vmem(edge_class.shape, jnp.int32), vmem(inverse.shape, jnp.bfloat16)]
-        + [vmem(whole, f32)] * 6
+        + [vmem(whole, f32)] * 4
         + [vmem(block, f32), vmem(block, f32), vmem(padded, f32), vmem(block, f32)]
-        + [vmem(padded, f32), vmem(block, f32)]
+        + [vmem(padded, f32)]
+        + [vmem((2, height, whole[2]), f32)] * 6
         + [vmem((height, width), f32)] * 4
         + [vmem((2, dates + 8, width), f32), vmem((2, dates, width), f32)] * 2
         + [vmem((2, height, LANES), f32)] * 4
         + [vmem((3, height, LANES), f32), vmem((3, most, height, LANES), f32)]
-        + [pltpu.SMEM((dates - 1,), f32), dma((6,)), dma((6, groups)), dma((6, groups)), dma((2, 4)), dma((2, 4))]
+        + [pltpu.SMEM((dates - 1,), f32), dma((6,)), dma((4, groups)), dma((4, groups))] + [dma((2, 4))] * 4
         + [dma((3, most)), dma((3, most))]
     )
     anywhere = pl.BlockSpec(memory_space=pltpu.HBM)

time: 56.2 us -> 53.6 us (0.954)
  Pallas kernels: 54 us -> 51.5 us
    pallas_call x1, Pallas kernels: 54 us -> 51.5 us  [body(): pl.pallas_call(functools.partial(kernel, rows, groups, low_size), out_sha...]
where the time goes in v4:
time: 53.6 us; the launch traced here: 53.5 us
  Pallas kernels  51.5 us (96%)
  local copies, waits for them, and re-layouts  1.41 us (3%)
  between operations  0.64 us (1%)
    pallas_call x1, Pallas kernels, body(): pl.pallas_call(functools.partial(kernel, rows, groups, low_size), out_sha...  51.5 us
    unnamed x2, local copies, waits for them, and re-layouts  1.41 us

profile of v4, /device:TPU:1, one launch (start us, length us, event | category | flops | bytes accessed | tf_op | source)
XLA Modules:
  0.0 53.5 jit_solution(6267129683130074090)
XLA Ops:
  0.6 51.5 %cg.1 = (f32[2,8,4096]{2,1,0:T(8,128)S(1)}, f32[2,8,4096]{2,1,0:T(8,128)S(1)}) custom-call(s32[2,8,4096]{2,1,0:T(8,128)} %mask_hbm.1, f32[2,8,4096]{2,1,0:T(8,128)} %prec_hbm.1, f32[2,8,4096]{2,1,0:T(8,128)} %obs_hbm.1, s32[2,8,4096]{2,1,0:T(8,128)} %edge_hbm.1, f32[15]{0:T(128)} %tau_hbm.1, bf16[16,16,8,512]{3,2,1,0:T(8,128)(2,1)} %inv_hbm.1), custom_call_target="tpu_custom_call" | custom-call | tf_op jit(solution)/shard_map/cg/pallas_call | solution.py:447
  52.1 0.7 %copy.10 = f32[2,8,4096]{2,1,0:T(8,128)} copy(f32[2,8,4096]{2,1,0:T(8,128)S(1)} %get-tuple-element.4) | data formatting | bytes 524288
  52.8 0.7 %copy.11 = f32[2,8,4096]{2,1,0:T(8,128)} copy(f32[2,8,4096]{2,1,0:T(8,128)S(1)} %get-tuple-element.5) | data formatting | bytes 524288

commit v5 on v4

--- a/solution.py
+++ b/solution.py
@@ -356,8 +356,15 @@
             sol_ref[date, :, span] = combined(
                 precond_date[date, :, span], mapped_date[date, :, span]
             )
-    for copy in precond_halo + mapped_halo:
+    for copy in precond_halo[:2] + mapped_halo[:2]:
         copy.wait_recv()
+
+    between = []
+    for date in range(dates_here + 1):
+        when = group * dates_here + date
+        inside = (when > 0) & (when < dates)
+        place = jnp.minimum(jnp.maximum(when - 1, 0), dates - 2)
+        between.append(jnp.where(inside, tau_ref[place], 0.0))
 
     for number, span in enumerate(spans):
         tile_before = slice(max(span.start - LANES, 0), max(span.start, LANES))
@@ -377,9 +384,6 @@
             pltpu.roll(under, 1, 0),
         )
         for date in range(dates_here):
-            when = group * dates_here + date
-            tau_up = jnp.where(when < dates - 1, tau_ref[jnp.minimum(when, dates - 2)], 0.0)
-            tau_down = jnp.where(when > 0, tau_ref[jnp.maximum(when - 1, 0)], 0.0)
             here = sol_ref[date, :, span]
             this = slice(date, date + 1)
             above = combined(from_above_date[0, this, span], from_above_date[1, this, span])
@@ -393,19 +397,25 @@
                 pltpu.roll(here, width - 1, 1),
                 pltpu.roll(sol_ref[date, :, tile_after], LANES - 1, 1),
             )
-            if date > 0:
-                before_here = sol_ref[date - 1, :, span]
-            else:
-                before_here = combined(from_before[0, :, span], from_before[1, :, span])
-            if date + 1 < dates_here:
-                after_here = sol_ref[date + 1, :, span]
-            else:
-                after_here = combined(from_after[0, :, span], from_after[1, :, span])
             out = (MASS + weight_date[date, :, span]) * here
             out = out + ahead * (here - right) + behind * (here - left)
             out = out + under * (here - below) + over * (here - above)
-            out = out + tau_up * (here - after_here) + tau_down * (here - before_here)
+            if date > 0:
+                out = out + between[date] * (here - sol_ref[date - 1, :, span])
+            if date + 1 < dates_here:
+                out = out + between[date + 1] * (here - sol_ref[date + 1, :, span])
             res_ref[date, :, span] = rhs_date[date, :, span] - out
+    for copy in precond_halo[2:] + mapped_halo[2:]:
+        copy.wait_recv()
+    for span in spans:
+        for date, weight_out, other in (
+            (0, between[0], from_before),
+            (dates_here - 1, between[dates_here], from_after),
+        ):
+            there = combined(other[0, :, span], other[1, :, span])
+            res_ref[date, :, span] = res_ref[date, :, span] - weight_out * (
+                sol_ref[date, :, span] - there
+            )
     back = (precond_copies, mapped_copies)
     for copies in (rhs_copies, weight_copies) + back:
         for sent, _ in copies:

time: 53.6 us -> 53.3 us (level)
  no operation moved by 1% of the time
where the time goes in v5:
time: 53.3 us; the launch traced here: 53.2 us
  Pallas kernels  51.1 us (96%)
  local copies, waits for them, and re-layouts  1.41 us (3%)
  between operations  0.64 us (1%)
    pallas_call x1, Pallas kernels, body(): pl.pallas_call(functools.partial(kernel, rows, groups, low_size), out_sha...  51.1 us
    unnamed x2, local copies, waits for them, and re-layouts  1.41 us

profile of v5, /device:TPU:1, one launch (start us, length us, event | category | flops | bytes accessed | tf_op | source)
XLA Modules:
  0.0 53.2 jit_solution(16621278237587842880)
XLA Ops:
  0.6 51.1 %cg.1 = (f32[2,8,4096]{2,1,0:T(8,128)S(1)}, f32[2,8,4096]{2,1,0:T(8,128)S(1)}) custom-call(s32[2,8,4096]{2,1,0:T(8,128)} %mask_hbm.1, f32[2,8,4096]{2,1,0:T(8,128)} %prec_hbm.1, f32[2,8,4096]{2,1,0:T(8,128)} %obs_hbm.1, s32[2,8,4096]{2,1,0:T(8,128)} %edge_hbm.1, f32[15]{0:T(128)} %tau_hbm.1, bf16[16,16,8,512]{3,2,1,0:T(8,128)(2,1)} %inv_hbm.1), custom_call_target="tpu_custom_call" | custom-call | tf_op jit(solution)/shard_map/cg/pallas_call | solution.py:457
  51.8 0.7 %copy.10 = f32[2,8,4096]{2,1,0:T(8,128)} copy(f32[2,8,4096]{2,1,0:T(8,128)S(1)} %get-tuple-element.4) | data formatting | bytes 524288
  52.5 0.7 %copy.11 = f32[2,8,4096]{2,1,0:T(8,128)} copy(f32[2,8,4096]{2,1,0:T(8,128)S(1)} %get-tuple-element.5) | data formatting | bytes 524288

commit v6 on v5

--- a/solution.py
+++ b/solution.py
@@ -8,7 +8,7 @@
 
 MASS = 0.1
 LANES = 128
-UNROLL = 4
+UNROLL = 8
 VMEM_BYTES = 16 * 1024 * 1024
 MESH = pl.DeviceIdType.MESH
 RHS, WEIGHT, PRECOND, MAPPED = range(4)

time: 53.3 us -> 52.6 us (0.987)
  Pallas kernels: 51.1 us -> 50.4 us
    pallas_call x1, Pallas kernels: 51.1 us -> 50.4 us  [body(): pl.pallas_call(functools.partial(kernel, rows, groups, low_size), out_sha...]
where the time goes in v6:
time: 52.6 us; the launch traced here: 52.4 us
  Pallas kernels  50.4 us (96%)
  local copies, waits for them, and re-layouts  1.41 us (3%)
  between operations  0.64 us (1%)
    pallas_call x1, Pallas kernels, body(): pl.pallas_call(functools.partial(kernel, rows, groups, low_size), out_sha...  50.4 us
    unnamed x2, local copies, waits for them, and re-layouts  1.41 us

profile of v6, /device:TPU:1, one launch (start us, length us, event | category | flops | bytes accessed | tf_op | source)
XLA Modules:
  0.0 52.4 jit_solution(6458645955628824088)
XLA Ops:
  0.6 50.4 %cg.1 = (f32[2,8,4096]{2,1,0:T(8,128)S(1)}, f32[2,8,4096]{2,1,0:T(8,128)S(1)}) custom-call(s32[2,8,4096]{2,1,0:T(8,128)} %mask_hbm.1, f32[2,8,4096]{2,1,0:T(8,128)} %prec_hbm.1, f32[2,8,4096]{2,1,0:T(8,128)} %obs_hbm.1, s32[2,8,4096]{2,1,0:T(8,128)} %edge_hbm.1, f32[15]{0:T(128)} %tau_hbm.1, bf16[16,16,8,512]{3,2,1,0:T(8,128)(2,1)} %inv_hbm.1), custom_call_target="tpu_custom_call" | custom-call | tf_op jit(solution)/shard_map/cg/pallas_call | solution.py:457
  51.0 0.7 %copy.10 = f32[2,8,4096]{2,1,0:T(8,128)} copy(f32[2,8,4096]{2,1,0:T(8,128)S(1)} %get-tuple-element.4) | data formatting | bytes 524288
  51.7 0.7 %copy.11 = f32[2,8,4096]{2,1,0:T(8,128)} copy(f32[2,8,4096]{2,1,0:T(8,128)S(1)} %get-tuple-element.5) | data formatting | bytes 524288
